TPU v7x, 512 devices: a whole 4x8x8 slice. The times are simulated.
512 devices in a mesh: rack: 32 (over x, y), expert: 16 (over z, core).
Axes of the slice: x: 4, y: 8, z: 8, core: 2. Of those that a mesh axis runs over, the one named last changes fastest.
Arguments:
- hidden_in: bfloat16 [512, 3584], P(('rack', 'expert')), may hold values from -6 to 6
- norm_gain: float32 [3584], replicated, may hold values from 0.1 to 1.9
- expert_ids: int32 [4, 512, 8], P(None, ('rack', 'expert')), may hold values from 0 to 31, all different within a row; in each aligned block of 16 rows (0 to 15, 16 to 31, ..., all dimensions but the last counted through in order) at most 6 rows name the same one
- gate_levels: int32 [4, 512, 8], P(None, ('rack', 'expert')), may hold values from 1 to 255
- w_gate_up: bfloat16 [32, 16, 1792, 2, 256], P('rack', 'expert'), may hold values from -0.09375 to 0.09375
- w_down: bfloat16 [32, 16, 256, 1792], P('rack', 'expert'), may hold values from -0.125 to 0.125
Outputs:
- hidden_out: float32 [512, 3584], P(('rack', 'expert'))
Inputs may be any that keep to these rules, and one draw needn't show every extreme that they name: `expert_ids`: each token names 8 different experts in each step; in each step at most 6 of the 16 tokens of one index of rack (an aligned block of the token order) name the same expert, and that many do in some blocks.
All inputs are finite; a program needn't handle non-finite values.
Results may differ from a plain program's by a relative error of at most 0.015.
Values may be sent and summed in bfloat16 or wider, within the bound.
A program may use at most 64 MiB of HBM per device.

v0:
```python
import jax
import jax.numpy as jnp
from jax import lax
from jax.sharding import PartitionSpec as P

TOP = 8
STEPS = 4


def swapped(shard, axis, bit):
    return lax.ppermute(shard, axis, [(i, i ^ 1 << bit) for i in range(lax.axis_size(axis))])


def per_device(hidden_in, norm_gain, expert_ids, gate_levels, w_gate_up, w_down):
    rack_count = lax.axis_size("rack")
    group_count = lax.axis_size("expert")
    group_index = lax.axis_index("expert")
    half_index = group_index % 2
    tok_rows = hidden_in.shape[0]
    rack_rows = tok_rows * group_count
    slot_count = min(rack_rows, 3 * rack_rows * TOP // (2 * rack_count))
    model_width = hidden_in.shape[1]
    half_width = model_width // 2
    part_width = w_down.shape[2]
    gate_up_weight = w_gate_up[0, 0].reshape(half_width, 2 * part_width)
    down_weight = w_down[0, 0]
    all_ids, all_levels = (
        lax.all_gather(expert_ids, "expert", axis=1, tiled=True),
        lax.all_gather(gate_levels, "expert", axis=1, tiled=True),
    )
    expert_range = jnp.arange(rack_count, dtype=jnp.int32)
    slot_ids = jnp.arange(slot_count, dtype=jnp.int32)
    residual = hidden_in.astype(jnp.float32)
    for step_index in range(STEPS):
        mean_square = jnp.mean(residual * residual, axis=-1, keepdims=True)
        normed = (residual * lax.rsqrt(mean_square + 1e-06) * norm_gain).astype(jnp.bfloat16)
        rack_normed = lax.all_gather(normed, "expert", axis=0, tiled=True)
        picked = all_ids[step_index]
        level_vals = all_levels[step_index].astype(jnp.float32)
        shares = level_vals / jnp.sum(level_vals, axis=-1, keepdims=True)
        matches = picked[:, :, None] == expert_range[None, None, :]
        chosen = jnp.sum(matches.astype(jnp.int32), axis=1)
        mixing = jnp.sum(jnp.where(matches, shares[:, :, None], jnp.float32(0.0)), axis=1).astype(
            jnp.bfloat16
        )
        slot_rank = jnp.cumsum(chosen, axis=0) - chosen
        placement = chosen[:, :, None] * (slot_rank[:, :, None] == slot_ids).astype(jnp.int32)
        dispatch_map = (
            jnp.transpose(placement, (1, 2, 0))
            .reshape(rack_count * slot_count, rack_rows)
            .astype(jnp.bfloat16)
        )
        outgoing = jnp.dot(dispatch_map, rack_normed, preferred_element_type=jnp.float32).astype(
            jnp.bfloat16
        )
        outgoing = outgoing.reshape(rack_count, slot_count, model_width)
        combine_map = (placement.astype(jnp.bfloat16) * mixing[:, :, None]).reshape(
            rack_rows, rack_count * slot_count
        )
        half_rows = lax.dynamic_slice_in_dim(outgoing, half_index * half_width, half_width, 2)
        slot_rows = lax.all_to_all(half_rows, "rack", split_axis=0, concat_axis=0, tiled=True)
        layout = slot_rows.shape
        flat_rows = slot_rows.reshape(-1, half_width)
        gate_up = jnp.dot(flat_rows, gate_up_weight, preferred_element_type=jnp.float32)
        gate_up = gate_up + swapped(gate_up.astype(jnp.bfloat16), "expert", 0).astype(gate_up.dtype)
        activated = (jax.nn.silu(gate_up[:, :part_width]) * gate_up[:, part_width:]).astype(
            jnp.bfloat16
        )
        partial_value = jnp.dot(activated, down_weight, preferred_element_type=jnp.float32).astype(
            jnp.bfloat16
        )
        partial_value = partial_value.reshape(layout)
        finished = lax.all_to_all(partial_value, "rack", split_axis=0, concat_axis=0, tiled=True)
        partial_sum = jnp.dot(
            combine_map, finished.reshape(-1, half_width), preferred_element_type=jnp.float32
        )
        full_sum = jnp.zeros((rack_rows, model_width), jnp.float32)
        full_sum = lax.dynamic_update_slice_in_dim(
            full_sum, partial_sum, half_index * half_width, 1
        )
        update = lax.psum_scatter(
            full_sum.astype(jnp.bfloat16), "expert", scatter_dimension=0, tiled=True
        ).astype(jnp.float32)
        residual = residual + update
    return residual


def solution(mesh):
    in_specs = (
        P(("rack", "expert"), None),
        P(),
        P(None, ("rack", "expert"), None),
        P(None, ("rack", "expert"), None),
        P("rack", "expert", None, None, None),
        P("rack", "expert", None, None),
    )
    out_specs = P(("rack", "expert"), None)
    return jax.shard_map(
        per_device, mesh=mesh, in_specs=in_specs, out_specs=out_specs, check_vma=False
    )
```

profile of v0, /device:TPU:1, one launch (start us, length us, event | category | flops | bytes accessed | tf_op | source)
XLA Modules:
  0.0 872.3 jit_solution(15694165037832759216)
XLA Ops:
  6.5 24.9 %all_gather.18 = s32[4,16,8]{2,0,1:T(4,128)S(1)} all-gather(s32[4,1,8]{2,0,1:T(4,128)} %bitcast.116), channel_id=1, replica_groups=mesh['rack'=32,'expert'=16] {'expert'}, dimensions={1}, use_global_device_ids=true | all-gather | bytes 2176 | tf_op jit(solution)/shard_map/all_gather | solution.py:28
  34.9 15.1 %all-gather = bf16[16,1,3584]{2,1,0:T(2,128)(2,1)S(1)} all-gather(bf16[1,1,3584]{2,1,0:T(2,128)(2,1)S(1)} %convert_bitcast_fusion.3), channel_id=1, replica_groups=mesh['rack'=32,'expert'=16] {'expert'}, dimensions={0}, use_global_device_ids=true | all-gather | bytes 121856 | tf_op jit(solution)/shard_map/all_gather | solution.py:37
  52.1 2.2 constant_dynamic-slice_fusion.3
  54.2 9.8 %all-to-all-start = ((bf16[32,6,1792]{2,1,0:T(8,128)(2,1)}), bf16[32,6,1792]{2,1,0:T(8,128)(2,1)}, u32[]{:S(2)}, u32[]{:S(2)}) async-start(bf16[32,6,1792]{2,1,0:T(8,128)(2,1)} %constant_dynamic-slice_fusion.3), calls=%async_computation | async-start | bytes 1835008 | tf_op jit(solution)/shard_map/all_to_all | solution.py:61
  65.9 21.0 %all-to-all-done = bf16[32,6,1792]{2,1,0:T(8,128)(2,1)} async-done(((bf16[32,6,1792]{2,1,0:T(8,128)(2,1)}), bf16[32,6,1792]{2,1,0:T(8,128)(2,1)}, u32[]{:S(2)}, u32[]{:S(2)}) %all-to-all-start) | async-done | bytes 688160 | tf_op jit(solution)/shard_map/all_to_all | solution.py:61
  88.8 5.7 collective-permute-start
  97.2 5.1 all-to-all-start.1
  102.4 16.4 %all_gather.19 = s32[4,16,8]{2,0,1:T(4,128)S(1)} all-gather(s32[4,1,8]{2,0,1:T(4,128)S(1)} %bitcast.117), channel_id=1, replica_groups=mesh['rack'=32,'expert'=16] {'expert'}, dimensions={1}, use_global_device_ids=true | all-gather | bytes 2176 | tf_op jit(solution)/shard_map/all_gather | solution.py:29
  119.2 5.4 all-to-all-done.1
  128.3 109.4 %all-reduce.9.cloned.1.call-done = bf16[16,3584]{1,0:T(8,128)(2,1)} async-done(((bf16[16,3584]{1,0:T(8,128)(2,1)}), bf16[16,3584]{1,0:T(8,128)(2,1)}) %all-reduce.9.cloned.1.call-update) | async-done | bytes 114704
  237.7 2.1 multiply_reduce_fusion.2
  240.6 15.4 %all-gather.1 = bf16[16,1,3584]{2,1,0:T(2,128)(2,1)S(1)} all-gather(bf16[1,1,3584]{2,1,0:T(2,128)(2,1)S(1)} %convert_bitcast_fusion.2), channel_id=1, replica_groups=mesh['rack'=32,'expert'=16] {'expert'}, dimensions={0}, use_global_device_ids=true | all-gather | bytes 121856 | tf_op jit(solution)/shard_map/all_gather | solution.py:37
  257.6 3.4 reshape.247
  262.2 32.1 %all_to_all.40 = bf16[32,6,1792]{2,1,0:T(8,128)(2,1)} all-to-all(bf16[32,6,1792]{2,1,0:T(8,128)(2,1)S(1)} %constant_dynamic-slice_fusion.2), channel_id=1, replica_groups=mesh['rack'=32,'expert'=16] {'rack'}, dimensions={0} | all-to-all | bytes 1376256 | tf_op jit(solution)/shard_map/all_to_all | solution.py:61
  296.2 5.7 collective-permute-start.1
  304.6 5.1 all-to-all-start.3
  310.2 21.8 %all-to-all-done.3 = bf16[32,6,1792]{2,1,0:T(8,128)(2,1)} async-done(((bf16[32,6,1792]{2,1,0:T(8,128)(2,1)}), bf16[32,6,1792]{2,1,0:T(8,128)(2,1)}, u32[]{:S(2)}, u32[]{:S(2)}) %all-to-all-start.3) | async-done | bytes 688160 | tf_op jit(solution)/shard_map/all_to_all | solution.py:73
  334.4 112.4 %all-reduce.11.cloned.1.call-done = bf16[16,3584]{1,0:T(8,128)(2,1)} async-done(((bf16[16,3584]{1,0:T(8,128)(2,1)}), bf16[16,3584]{1,0:T(8,128)(2,1)}) %all-reduce.11.cloned.1.call-update) | async-done | bytes 114704
  449.7 15.4 %all-gather.2 = bf16[16,1,3584]{2,1,0:T(2,128)(2,1)S(1)} all-gather(bf16[1,1,3584]{2,1,0:T(2,128)(2,1)S(1)} %convert_bitcast_fusion.1), channel_id=1, replica_groups=mesh['rack'=32,'expert'=16] {'expert'}, dimensions={0}, use_global_device_ids=true | all-gather | bytes 121856 | tf_op jit(solution)/shard_map/all_gather | solution.py:37
  466.7 3.4 reshape.250
  471.3 32.1 %all_to_all.41 = bf16[32,6,1792]{2,1,0:T(8,128)(2,1)} all-to-all(bf16[32,6,1792]{2,1,0:T(8,128)(2,1)S(1)} %constant_dynamic-slice_fusion.1), channel_id=1, replica_groups=mesh['rack'=32,'expert'=16] {'rack'}, dimensions={0} | all-to-all | bytes 1376256 | tf_op jit(solution)/shard_map/all_to_all | solution.py:61
  505.3 5.7 collective-permute-start.2
  513.7 5.1 all-to-all-start.5
  519.3 21.8 %all-to-all-done.5 = bf16[32,6,1792]{2,1,0:T(8,128)(2,1)} async-done(((bf16[32,6,1792]{2,1,0:T(8,128)(2,1)}), bf16[32,6,1792]{2,1,0:T(8,128)(2,1)}, u32[]{:S(2)}, u32[]{:S(2)}) %all-to-all-start.5) | async-done | bytes 688160 | tf_op jit(solution)/shard_map/all_to_all | solution.py:73
  543.5 112.5 %all-reduce.13.cloned.1.call-done = bf16[16,3584]{1,0:T(8,128)(2,1)} async-done(((bf16[16,3584]{1,0:T(8,128)(2,1)}), bf16[16,3584]{1,0:T(8,128)(2,1)}) %all-reduce.13.cloned.1.call-update) | async-done | bytes 114704
  658.8 15.4 %all-gather.3 = bf16[16,1,3584]{2,1,0:T(2,128)(2,1)S(1)} all-gather(bf16[1,1,3584]{2,1,0:T(2,128)(2,1)S(1)} %convert_bitcast_fusion), channel_id=1, replica_groups=mesh['rack'=32,'expert'=16] {'expert'}, dimensions={0}, use_global_device_ids=true | all-gather | bytes 121856 | tf_op jit(solution)/shard_map/all_gather | solution.py:37
  675.8 3.4 reshape.253
  680.4 32.1 %all_to_all.42 = bf16[32,6,1792]{2,1,0:T(8,128)(2,1)} all-to-all(bf16[32,6,1792]{2,1,0:T(8,128)(2,1)S(1)} %constant_dynamic-slice_fusion), channel_id=1, replica_groups=mesh['rack'=32,'expert'=16] {'rack'}, dimensions={0} | all-to-all | bytes 1376256 | tf_op jit(solution)/shard_map/all_to_all | solution.py:61
  714.4 5.7 collective-permute-start.3
  722.7 4.9 all-to-all-start.7
  728.0 21.9 %all-to-all-done.7 = bf16[32,6,1792]{2,1,0:T(8,128)(2,1)S(1)} async-done(((bf16[32,6,1792]{2,1,0:T(8,128)(2,1)}), bf16[32,6,1792]{2,1,0:T(8,128)(2,1)S(1)}, u32[]{:S(2)}, u32[]{:S(2)}) %all-to-all-start.7) | async-done | bytes 688160 | tf_op jit(solution)/shard_map/all_to_all | solution.py:73
  750.9 112.9 %all-reduce.15.cloned.1.call-done = bf16[16,3584]{1,0:T(8,128)(2,1)} async-done(((bf16[16,3584]{1,0:T(8,128)(2,1)}), bf16[16,3584]{1,0:T(8,128)(2,1)}) %all-reduce.15.cloned.1.call-update) | async-done | bytes 114704
  (146 shorter events, 50.6 us)
Async XLA Ops:
  6.5 89.1 %copy-start = (bf16[1,1,256,1792]{3,2,1,0:T(8,128)(2,1)S(1)}, bf16[1,1,256,1792]{3,2,1,0:T(8,128)(2,1)}, u32[]{:S(2)}) copy-start(bf16[1,1,256,1792]{3,2,1,0:T(8,128)(2,1)} %param.11) | copy-start | bytes 2752516
  32.0 20.1 %copy-start.7 = (s32[192]{0:T(256)}, s32[192]{0:T(256)S(1)}, u32[]{:S(2)}) copy-start(s32[192]{0:T(256)S(1)} %eq.180) | copy-start | bytes 2308
  54.2 32.7 %all-to-all-start = ((bf16[32,6,1792]{2,1,0:T(8,128)(2,1)}), bf16[32,6,1792]{2,1,0:T(8,128)(2,1)}, u32[]{:S(2)}, u32[]{:S(2)}) async-start(bf16[32,6,1792]{2,1,0:T(8,128)(2,1)} %constant_dynamic-slice_fusion.3), calls=%async_computation | async-start | bytes 1835008 | tf_op jit(solution)/shard_map/all_to_all | solution.py:61
  88.8 6.8 collective-permute-start
  96.0 6.4 copy-start.11
  97.2 140.5 %copy-start.6 = (bf16[1,3584]{1,0:T(2,128)(2,1)S(1)}, bf16[1,3584]{1,0:T(2,128)(2,1)}, u32[]{:S(2)}) copy-start(bf16[1,3584]{1,0:T(2,128)(2,1)} %param.6) | copy-start | bytes 21508
  97.2 143.3 %copy-start.5 = (f32[3584]{0:T(1024)S(1)}, f32[3584]{0:T(1024)}, u32[]{:S(2)}) copy-start(f32[3584]{0:T(1024)} %param.7) | copy-start | bytes 43012
  97.2 158.7 %copy-start.8 = (s32[192]{0:T(256)S(1)}, s32[192]{0:T(256)}, u32[]{:S(2)}) copy-start(s32[192]{0:T(256)} %copy-done.7) | copy-start | bytes 2308
  97.2 27.4 %all-to-all-start.1 = ((bf16[32,6,1792]{2,1,0:T(8,128)(2,1)}), bf16[32,6,1792]{2,1,0:T(8,128)(2,1)}, u32[]{:S(2)}, u32[]{:S(2)}) async-start(bf16[32,6,1792]{2,1,0:T(8,128)(2,1)} %reshape.246), calls=%async_computation.1 | async-start | bytes 1835008 | tf_op jit(solution)/shard_map/all_to_all | solution.py:73
  102.3 135.3 %all-reduce.9.cloned.1.call-start = ((), (), s32[]{:S(2)}) async-start(), calls=%async_computation.8 | async-start | bytes 229376
  126.1 0.7 copy-start.2
  296.2 6.8 collective-permute-start.1
  304.6 160.4 %copy-start.9 = (s32[192]{0:T(256)S(1)}, s32[192]{0:T(256)}, u32[]{:S(2)}) copy-start(s32[192]{0:T(256)} %copy-done.7) | copy-start | bytes 2308
  304.6 27.4 %all-to-all-start.3 = ((bf16[32,6,1792]{2,1,0:T(8,128)(2,1)}), bf16[32,6,1792]{2,1,0:T(8,128)(2,1)}, u32[]{:S(2)}, u32[]{:S(2)}) async-start(bf16[32,6,1792]{2,1,0:T(8,128)(2,1)} %reshape.249), calls=%async_computation.3 | async-start | bytes 1835008 | tf_op jit(solution)/shard_map/all_to_all | solution.py:73
  309.7 137.1 %all-reduce.11.cloned.1.call-start = ((), (), s32[]{:S(2)}) async-start(), calls=%async_computation.9 | async-start | bytes 229376
  333.4 0.7 copy-start.3
  505.3 6.8 collective-permute-start.2
  513.7 160.4 %copy-start.10 = (s32[192]{0:T(256)S(1)}, s32[192]{0:T(256)}, u32[]{:S(2)}) copy-start(s32[192]{0:T(256)} %copy-done.7) | copy-start | bytes 2308
  513.7 27.4 %all-to-all-start.5 = ((bf16[32,6,1792]{2,1,0:T(8,128)(2,1)}), bf16[32,6,1792]{2,1,0:T(8,128)(2,1)}, u32[]{:S(2)}, u32[]{:S(2)}) async-start(bf16[32,6,1792]{2,1,0:T(8,128)(2,1)} %reshape.252), calls=%async_computation.5 | async-start | bytes 1835008 | tf_op jit(solution)/shard_map/all_to_all | solution.py:73
  518.8 137.1 %all-reduce.13.cloned.1.call-start = ((), (), s32[]{:S(2)}) async-start(), calls=%async_computation.10 | async-start | bytes 229376
  542.5 0.7 copy-start.4
  714.4 6.8 collective-permute-start.3
  722.7 27.2 %all-to-all-start.7 = ((bf16[32,6,1792]{2,1,0:T(8,128)(2,1)}), bf16[32,6,1792]{2,1,0:T(8,128)(2,1)S(1)}, u32[]{:S(2)}, u32[]{:S(2)}) async-start(bf16[32,6,1792]{2,1,0:T(8,128)(2,1)} %reshape.255), calls=%async_computation.7 | async-start | bytes 1835008 | tf_op jit(solution)/shard_map/all_to_all | solution.py:73
  727.6 136.2 %all-reduce.15.cloned.1.call-start = ((), (), s32[]{:S(2)}) async-start(), calls=%async_computation.11 | async-start | bytes 229376
  750.2 0.7 copy-start.1
Sparse Core Ops, SparseCore 0:
  126.9 110.7 all-reduce.8
  334.2 112.5 all-reduce.10
  543.3 112.5 all-reduce.12
  751.0 112.7 all-reduce.14
where the time goes:
time: 874 us; the launch traced here: 872 us
  waiting for transfers between devices  543 us (62%)
  blocking collectives  199 us (23%)
  starting transfers between devices  52.9 us (6%)
  local copies, waits for them, and re-layouts  35.2 us (4%)
  between operations  16.6 us (2%)
  matrix products  13.6 us (2%)
  other arithmetic  11.8 us (1%)
    unnamed x8, waiting for transfers between devices  447 us
    all_to_all x3, blocking collectives, per_device(): lax.all_to_all(half_rows, 'rack', split_axis=0, concat_axis=0, tiled=True)  96.2 us
    all_to_all x4, waiting for transfers between devices, per_device(): lax.all_to_all(partial_value, 'rack', split_axis=0, concat_axis=0, tiled=...  70.9 us
    all_gather x4, blocking collectives, per_device(): rack_normed = lax.all_gather(normed, 'expert', axis=0, tiled=True)  61.1 us
    all_gather x1, blocking collectives, per_device(): lax.all_gather(expert_ids, 'expert', axis=1, tiled=True)  24.9 us
    ppermute x4, starting transfers between devices, swapped(): lax.ppermute(shard, axis, [(i, i ^ 1 << bit) for i in range(lax.axis_size...  22.9 us
    all_to_all x1, waiting for transfers between devices, per_device(): lax.all_to_all(half_rows, 'rack', split_axis=0, concat_axis=0, tiled=True)  21 us
    all_to_all x4, starting transfers between devices, per_device(): lax.all_to_all(partial_value, 'rack', split_axis=0, concat_axis=0, tiled=...  20.1 us
  transfers between devices with their start and end apart: 13, of which 13 were waited for; matrix products, arithmetic and copies ran while one was open for 1% of the time, Pallas kernels for 0%

commit v1 on v0

v1 whole, which is shorter than its diff:
```python
import functools

import jax
import jax.numpy as jnp
from jax import lax
from jax.experimental import pallas as pl
from jax.experimental.pallas import tpu as pltpu
from jax.sharding import PartitionSpec as P

MESH = pl.DeviceIdType.MESH
BF16 = jnp.bfloat16
F32 = jnp.float32
TILE = 128
GRID = (4, 8, 8)
ORDERS = (("y", "x", "z"), ("y", "z", "x"), ("z", "x", "y"))
STORED = ("z", "y", "x")


def shares_of(tiles):
    first = (tiles + 1) // 3
    second = (tiles + 1 - first) // 2
    return (first - 1, second, tiles + 1 - first - second)


def kernel(
    grid, steps, top, experts, widths,
    hid_ref, gain_ref, ids_ref, lev_ref, wgu_ref, wd_ref, out_ref,
    ga, gb, gc, pa, pb, pc, gu_ref, act_ref, xs_ref, xr_ref,
    res_ref, mix_ref, mixs_ref, mixr_ref, hs_ref, hr_ref, fs_ref, fr_ref, sss_ref, ssr_ref,
    rr_a, rr_b, rr_c, st_a, st_b, st_c, u_a, u_b, u_c, v_a, v_b, v_c, w_a, w_b, w_c, t_a, t_b, t_c,
    ag_send, ag_recv, rs_send, rs_recv, pair_send, pair_recv,
):
    size = dict(zip("xyz", grid))
    rack, col = lax.axis_index("rack"), lax.axis_index("expert")
    here = {"x": rack // size["y"], "y": rack % size["y"], "z": col // 2}
    core = col % 2
    half = sum(widths)
    tokens = 2 * grid[0] * grid[1] * grid[2]
    starts = (0, widths[0], widths[0] + widths[1])
    gathered, partial = (ga, gb, gc), (pa, pb, pc)
    ring_in, ring_out = (rr_a, rr_b, rr_c), (st_a, st_b, st_c)
    mid_out, mid_in = (u_a, u_b, u_c), (v_a, v_b, v_c)
    last_out, last_in = (w_a, w_b, w_c), (t_a, t_b, t_c)

    def device(at):
        return (at["x"] * size["y"] + at["y"], at["z"] * 2 + core)

    def away(axis, shift):
        n = size[axis]
        return lax.rem(here[axis] + (shift + n) % n, n)

    def moved(axis, shift):
        return device({**here, axis: away(axis, shift)})

    mate = (rack, col + 1 - 2 * core)

    def where_at(full, axis=None, at=None):
        return tuple(
            pl.ds(0, size[a]) if a in full else (at if a == axis else here[a]) for a in STORED
        )

    def to_mate(src, dst, slot):
        return pltpu.make_async_remote_copy(
            src_ref=src, dst_ref=dst, send_sem=pair_send.at[slot], recv_sem=pair_recv.at[slot],
            device_id=mate, device_id_type=MESH,
        )

    barrier = pltpu.get_barrier_semaphore()
    partners = [mate] + [moved(a, d) for a in "xyz" for d in range(1, size[a])]
    for partner in partners:
        pl.semaphore_signal(barrier, inc=1, device_id=partner, device_id_type=MESH)

    own = hid_ref[...].astype(F32)
    low, high = own[:, :half], own[:, half:]
    first_core = core == 0
    hs_ref[...] = jnp.where(first_core, high, low)
    levels = lev_ref[...].astype(F32)
    shares = levels / jnp.sum(levels, axis=-1, keepdims=True)
    chosen = ids_ref[...]
    lanes = lax.broadcasted_iota(jnp.int32, (steps, TILE), 1)
    mixing = jnp.zeros((steps, TILE), F32)
    for k in range(top):
        mixing += jnp.where(lanes == chosen[:, k : k + 1], shares[:, k : k + 1], 0.0)
    mixs_ref[...] = mixing
    pl.semaphore_wait(barrier, len(partners))
    sent = [to_mate(hs_ref, hr_ref, 0), to_mate(mixs_ref, mixr_ref, 1)]
    for copy in sent:
        copy.start()
    for copy in sent:
        copy.wait()
    row = lax.broadcasted_iota(jnp.int32, (2, half), 0)
    res_ref[...] = jnp.where(row == core, jnp.where(first_core, low, high), hr_ref[...])
    mix_row = lax.broadcasted_iota(jnp.int32, (2, TILE), 0)
    for s in range(steps):
        mix_ref[s] = jnp.where(mix_row == core, mixing[s : s + 1], mixr_ref[s : s + 1, :])
    gains = gain_ref[...]
    gain = jnp.where(first_core, gains[:, :half], gains[:, half:])

    def ag_copy(o, phase, slot, axis, full, at, shift):
        ref = gathered[o].at[where_at(full, axis, at)]
        return pltpu.make_async_remote_copy(
            src_ref=ref, dst_ref=ref, send_sem=ag_send.at[o, phase, slot],
            recv_sem=ag_recv.at[o, phase, slot], device_id=moved(axis, shift), device_id_type=MESH,
        )

    def rs_copy(o, phase, slot, src, dst, axis, shift):
        return pltpu.make_async_remote_copy(
            src_ref=src, dst_ref=dst, send_sem=rs_send.at[o, phase, slot],
            recv_sem=rs_recv.at[o, phase, slot], device_id=moved(axis, shift), device_id_type=MESH,
        )

    def ring_counts(axis):
        n = size[axis]
        return n // 2, n - 1 - n // 2

    def one_step(step, carry):
        residual = res_ref[...]
        sss_ref[...] = jnp.broadcast_to(
            jnp.sum(residual * residual, axis=-1, keepdims=True), sss_ref.shape
        )
        copy = to_mate(sss_ref, ssr_ref, 2)
        copy.start()
        copy.wait()
        total = (sss_ref[...] + ssr_ref[...])[:, :1]
        normed = (residual * lax.rsqrt(total / (2 * half) + 1e-6) * gain).astype(BF16)
        for o in range(3):
            block = normed[:, starts[o] : starts[o] + widths[o]]
            if o == 0:
                block = jnp.concatenate([block, mix_ref[step].astype(BF16)], axis=1)
            gathered[o][where_at(())] = block

        sends = []
        for phase in range(2):
            flying = []
            for o in range(3):
                if phase:
                    for copy in waits[o]:
                        copy.wait_recv()
                axis, full = ORDERS[o][phase], ORDERS[o][:phase]
                flying.append([
                    ag_copy(o, phase, d - 1, axis, full, here[axis], d)
                    for d in sorted(range(1, size[axis]), key=lambda d: -min(d, size[axis] - d))
                ])
                for copy in flying[o]:
                    copy.start()
                sends += flying[o]
            waits = flying
        rounds = max(size[o[2]] // 2 for o in ORDERS)
        for t in range(1, rounds + 1):
            flying = []
            for o in range(3):
                for copy in waits[o]:
                    copy.wait_recv()
                axis, full = ORDERS[o][2], ORDERS[o][:2]
                right, left = ring_counts(axis)
                copies = []
                if t <= right:
                    copies.append(ag_copy(o, 2, t - 1, axis, full, away(axis, 1 - t), 1))
                if t <= left:
                    copies.append(ag_copy(o, 2, right + t - 1, axis, full, away(axis, t - 1), -1))
                for copy in copies:
                    copy.start()
                sends += copies
                flying.append(copies)
            waits = flying
        for o in range(3):
            for copy in waits[o]:
                copy.wait_recv()

        chunk = tokens // size["z"]
        swaps = []
        for z in range(size["z"]):
            rows = pl.ds(z * chunk, chunk)
            total = None
            for o in range(3):
                x = gathered[o][z].reshape(chunk, gathered[o].shape[-1])[:, : widths[o]]
                part = jnp.dot(
                    x, wgu_ref[starts[o] : starts[o] + widths[o], :], preferred_element_type=F32
                )
                total = part if total is None else total + part
            gu_ref[rows, :] = total
            xs_ref[rows, :] = total.astype(BF16)
            swap = to_mate(xs_ref.at[rows], xr_ref.at[rows], 3 + z)
            swap.start()
            swaps.append(swap)
        hidden = wd_ref.shape[0]
        mine = (
            lax.broadcasted_iota(jnp.int32, (tokens, TILE), 1) == rack
        )
        weight = jnp.sum(
            jnp.where(mine, ga[..., widths[0] :].reshape(tokens, TILE).astype(F32), 0.0),
            axis=-1, keepdims=True,
        )
        for z in range(size["z"]):
            rows = pl.ds(z * chunk, chunk)
            swaps[z].wait()
            both = gu_ref[rows, :] + xr_ref[rows, :].astype(F32)
            gate, up = both[:, :hidden], both[:, hidden:]
            act_ref[rows, :] = (gate / (1.0 + jnp.exp(-gate)) * up).astype(BF16)
        for copy in sends:
            copy.wait_send()
        for o in range(3):
            part = jnp.dot(
                act_ref[...], wd_ref[:, starts[o] : starts[o] + widths[o]],
                preferred_element_type=F32,
            )
            partial[o][...] = (part * weight).astype(BF16).reshape(partial[o].shape)

        sends = []
        waits = [[], [], []]
        for t in range(1, rounds + 1):
            flying = []
            for o in range(3):
                axis, full = ORDERS[o][2], ORDERS[o][:2]
                right, left = ring_counts(axis)
                copies = []
                for count, base, sign in ((right, 0, 1), (left, right, -1)):
                    if t > count:
                        continue
                    slot = base + t - 1
                    at = where_at(full, axis, away(axis, sign * (count - t + 1)))
                    if t == 1:
                        src = partial[o].at[at]
                    else:
                        waits[o][0 if sign > 0 else 1].wait_recv()
                        ring_out[o][slot] = ring_in[o][slot - 1] + partial[o][at]
                        src = ring_out[o].at[slot]
                    copy = rs_copy(o, 0, slot, src, ring_in[o].at[slot], axis, sign)
                    copy.start()
                    copies.append(copy)
                sends += copies
                if waits[o] and len(copies) < len(waits[o]):
                    copies = copies + waits[o][len(copies):]
                flying.append(copies)
            waits = flying
        for o in range(3):
            axis, full = ORDERS[o][2], ORDERS[o][:2]
            right, left = ring_counts(axis)
            for copy in waits[o]:
                copy.wait_recv()
            total = partial[o][where_at(full, axis, here[axis])].astype(F32)
            total += ring_in[o][right - 1].astype(F32)
            if left:
                total += ring_in[o][right + left - 1].astype(F32)
            mid_out[o][...] = total.astype(BF16)

        flying = []
        for o in range(3):
            axis = ORDERS[o][1]
            other = [a for a in STORED if a in ORDERS[o][:2]]
            copies = []
            for d in range(1, size[axis]):
                at = tuple(
                    away(axis, d) if a == axis else pl.ds(0, size[a]) for a in other
                )
                copies.append(
                    rs_copy(o, 1, d - 1, mid_out[o].at[at], mid_in[o].at[d - 1], axis, d)
                )
            for copy in copies:
                copy.start()
            sends += copies
            flying.append(copies)
        waits = flying
        flying = []
        for o in range(3):
            axis = ORDERS[o][1]
            other = [a for a in STORED if a in ORDERS[o][:2]]
            at = tuple(here[axis] if a == axis else pl.ds(0, size[a]) for a in other)
            total = mid_out[o][at].astype(F32)
            for d in range(1, size[axis]):
                waits[o][d - 1].wait_recv()
                total += mid_in[o][d - 1].astype(F32)
            last_out[o][...] = total.astype(BF16)
            axis = ORDERS[o][0]
            copies = [
                rs_copy(o, 2, d - 1, last_out[o].at[away(axis, d)], last_in[o].at[d - 1], axis, d)
                for d in range(1, size[axis])
            ]
            for copy in copies:
                copy.start()
            sends += copies
            flying.append(copies)
        waits = flying
        for o in range(3):
            axis = ORDERS[o][0]
            total = last_out[o][here[axis]].astype(F32)
            for d in range(1, size[axis]):
                waits[o][d - 1].wait_recv()
                total += last_in[o][d - 1].astype(F32)
            res_ref[:, starts[o] : starts[o] + widths[o]] += total
        for copy in sends:
            copy.wait_send()
        return carry

    lax.fori_loop(0, steps, one_step, 0)

    residual = res_ref[...]
    fs_ref[...] = jnp.where(first_core, residual[1:2], residual[0:1])
    copy = to_mate(fs_ref, fr_ref, 2)
    copy.start()
    kept = jnp.where(first_core, residual[0:1], residual[1:2])
    copy.wait()
    out_ref[:, :half] = jnp.where(first_core, kept, fr_ref[...])
    out_ref[:, half:] = jnp.where(first_core, fr_ref[...], kept)


def per_device(grid, hidden_in, norm_gain, expert_ids, gate_levels, w_gate_up, w_down):
    steps, _, top = expert_ids.shape
    width = hidden_in.shape[1]
    half = width // 2
    hidden = w_down.shape[2]
    tokens = 2 * grid[0] * grid[1] * grid[2]
    widths = tuple(TILE * n for n in shares_of(half // TILE))
    size = dict(zip("xyz", grid))
    stored = tuple(size[a] for a in STORED)

    def dims(names):
        return tuple(size[a] for a in STORED if a in names)

    scratch = [pltpu.VMEM(stored + (2, w + (TILE if o == 0 else 0)), BF16) for o, w in enumerate(widths)]
    scratch += [pltpu.VMEM(stored + (2, w), BF16) for w in widths]
    scratch += [
        pltpu.VMEM((tokens, 2 * hidden), F32),
        pltpu.VMEM((tokens, hidden), BF16),
        pltpu.VMEM((tokens, 2 * hidden), BF16),
        pltpu.VMEM((tokens, 2 * hidden), BF16),
        pltpu.VMEM((2, half), F32),
        pltpu.VMEM((steps, 2, TILE), F32),
        pltpu.VMEM((steps, TILE), F32),
        pltpu.VMEM((steps, TILE), F32),
        pltpu.VMEM((1, half), F32),
        pltpu.VMEM((1, half), F32),
        pltpu.VMEM((1, half), F32),
        pltpu.VMEM((1, half), F32),
        pltpu.VMEM((2, TILE), F32),
        pltpu.VMEM((2, TILE), F32),
    ]
    for _ in range(2):
        scratch += [
            pltpu.VMEM((size[o[2]] - 1,) + dims(o[:2]) + (2, w), BF16) for o, w in zip(ORDERS, widths)
        ]
    scratch += [pltpu.VMEM(dims(o[:2]) + (2, w), BF16) for o, w in zip(ORDERS, widths)]
    scratch += [
        pltpu.VMEM((size[o[1]] - 1, size[o[0]], 2, w), BF16) for o, w in zip(ORDERS, widths)
    ]
    scratch += [pltpu.VMEM((size[o[0]], 2, w), BF16) for o, w in zip(ORDERS, widths)]
    scratch += [pltpu.VMEM((size[o[0]] - 1, 2, w), BF16) for o, w in zip(ORDERS, widths)]
    most = max(grid) - 1
    scratch += [pltpu.SemaphoreType.DMA((3, 3, most))] * 4
    scratch += [pltpu.SemaphoreType.DMA((3 + size["z"],))] * 2
    return pl.pallas_call(
        functools.partial(kernel, grid, steps, top, 0, widths),
        out_shape=jax.ShapeDtypeStruct((1, width), F32),
        in_specs=[pl.BlockSpec(memory_space=pltpu.VMEM)] * 6,
        out_specs=pl.BlockSpec(memory_space=pltpu.VMEM),
        scratch_shapes=scratch,
        compiler_params=pltpu.CompilerParams(
            collective_id=0, has_side_effects=True, vmem_limit_bytes=48 << 20
        ),
    )(
        hidden_in,
        norm_gain.reshape(1, width),
        expert_ids[:, 0, :],
        gate_levels[:, 0, :],
        w_gate_up[0, 0].reshape(half, 2 * hidden),
        w_down[0, 0],
    )


def solution(mesh, grid=GRID):
    in_specs = (
        P(("rack", "expert"), None),
        P(),
        P(None, ("rack", "expert"), None),
        P(None, ("rack", "expert"), None),
        P("rack", "expert", None, None, None),
        P("rack", "expert", None, None),
    )
    out_specs = P(("rack", "expert"), None)
    return jax.shard_map(
        functools.partial(per_device, grid),
        mesh=mesh, in_specs=in_specs, out_specs=out_specs, check_vma=False,
    )
```

time: 874 us -> 278 us (0.32)
  waiting for transfers between devices: 543 us -> 0 us
  Pallas kernels: 0 us -> 274 us
  blocking collectives: 199 us -> 0 us
  starting transfers between devices: 52.9 us -> 0 us
  local copies, waits for them, and re-layouts: 35.2 us -> 3.31 us
  between operations: 16.6 us -> 0.08 us
  matrix products: 13.6 us -> 0 us
  other arithmetic: 11.8 us -> 0 us
    unnamed x8 -> x0, waiting for transfers between devices: 447 us -> none
    pallas_call x0 -> x1, Pallas kernels: none -> 274 us  [per_device(): pl.pallas_call(functools.partial(kernel, grid, steps, top, 0, widths), ou...]
    all_gather x6 -> x0, blocking collectives: 102 us -> none  [the longest x4 61.1 us: per_device(): rack_normed = lax.all_gather(normed, 'expert', axis=0, tiled=True)]
    all_to_all x3 -> x0, blocking collectives: 96.2 us -> none  [per_device(): lax.all_to_all(half_rows, 'rack', split_axis=0, concat_axis=0, tiled=True)]
    all_to_all x5 -> x0, waiting for transfers between devices: 91.9 us -> none  [the longest x4 70.9 us: per_device(): lax.all_to_all(partial_value, 'rack', split_axis=0, concat_axis=0, tiled=...]
    all_to_all x5 -> x0, starting transfers between devices: 29.9 us -> none  [the longest x4 20.1 us: per_device(): lax.all_to_all(partial_value, 'rack', split_axis=0, concat_axis=0, tiled=...]
    ppermute x4 -> x0, starting transfers between devices: 22.9 us -> none  [swapped(): lax.ppermute(shard, axis, [(i, i ^ 1 << bit) for i in range(lax.axis_size...]
    reshape x12 -> x1, local copies, waits for them, and re-layouts: 21.9 us -> 0.73 us  [per_device(): norm_gain.reshape(1, width)]
  transfers between devices with their start and end apart: 13 -> 0, of which waited for: 13 -> 0; matrix products, arithmetic and copies ran while one was open for 1% -> 0% of each run, Pallas kernels for 0% -> 0%
where the time goes in v1:
time: 278 us
  Pallas kernels  274 us (99%)
  local copies, waits for them, and re-layouts  3.31 us (1%)
    pallas_call x1, Pallas kernels, per_device(): pl.pallas_call(functools.partial(kernel, grid, steps, top, 0, widths), ou...  274 us

profile of v1, /device:TPU:1, one launch (start us, length us, event | category | flops | bytes accessed | tf_op | source)
XLA Modules:
  0.0 277.7 jit_solution(12603643762050424321)
XLA Ops:
  0.0 0.7 reshape.3.gain_ref
  0.7 0.0 copy-start
  0.7 0.0 copy-start.1
  0.8 0.0 copy-start.2
  0.8 0.0 copy-start.3
  0.8 2.0 copy.7
  2.7 0.0 copy-done
  2.8 0.0 copy-done.1
  2.8 0.0 copy-done.2
  2.8 0.0 copy-done.3
  2.8 274.4 %shard_map.64 = f32[1,3584]{1,0:T(1,128)S(1)} custom-call(bf16[1,3584]{1,0:T(2,128)(2,1)S(1)} %copy-done.1, f32[1,3584]{1,0:T(1,128)S(1)} %reshape.3.gain_ref, s32[4,8]{1,0:T(4,128)S(1)} %bitcast.8, s32[4,8]{1,0:T(4,128)S(1)} %bitcast.9, bf16[1792,512]{1,0:T(8,128)(2,1)S(1)} %bitcast.6, bf16[256,1792]{1,0:T(8,128)(2,1)S(1)} %bitcast.7), custom_call_target="tpu_custom_call" | custom-call | tf_op jit(solution)/shard_map/pallas_call | solution.py:351
  277.1 0.6 copy.9
Async XLA Ops:
  0.7 2.0 copy-start
  0.7 2.0 copy-start.1
  0.8 2.0 copy-start.2
  0.8 2.0 copy-start.3

commit v2 on v1

--- a/solution.py
+++ b/solution.py
@@ -14,6 +14,10 @@
 GRID = (4, 8, 8)
 ORDERS = (("y", "x", "z"), ("y", "z", "x"), ("z", "x", "y"))
 STORED = ("z", "y", "x")
+LONG = 8
+SIDES = ((0, 1), (6, -1))
+SEQUENCE = (0, 2, 1)
+LANDING = (1, 0, 2)
 
 
 def shares_of(tiles):
@@ -54,10 +58,21 @@
 
     mate = (rack, col + 1 - 2 * core)
 
-    def where_at(full, axis=None, at=None):
-        return tuple(
-            pl.ds(0, size[a]) if a in full else (at if a == axis else here[a]) for a in STORED
-        )
+    def span(names, part):
+        lead = [a for a in STORED if a in names][:1]
+        spans = {a: pl.ds(0, size[a]) for a in names}
+        if part is not None:
+            long = size[lead[0]] // 2
+            spans[lead[0]] = pl.ds(part * long, long)
+        return spans
+
+    def where_at(full, axis=None, at=None, part=None):
+        spans = span(full, part)
+        return tuple(spans[a] if a in full else (at if a == axis else here[a]) for a in STORED)
+
+    def inner(full, part=None):
+        spans = span(full, part)
+        return tuple(spans[a] for a in STORED if a in full)
 
     def to_mate(src, dst, slot):
         return pltpu.make_async_remote_copy(
@@ -96,8 +111,8 @@
     gains = gain_ref[...]
     gain = jnp.where(first_core, gains[:, :half], gains[:, half:])
 
-    def ag_copy(o, phase, slot, axis, full, at, shift):
-        ref = gathered[o].at[where_at(full, axis, at)]
+    def ag_copy(o, phase, slot, axis, full, at, shift, part=None):
+        ref = gathered[o].at[where_at(full, axis, at, part)]
         return pltpu.make_async_remote_copy(
             src_ref=ref, dst_ref=ref, send_sem=ag_send.at[o, phase, slot],
             recv_sem=ag_recv.at[o, phase, slot], device_id=moved(axis, shift), device_id_type=MESH,
@@ -108,10 +123,6 @@
             src_ref=src, dst_ref=dst, send_sem=rs_send.at[o, phase, slot],
             recv_sem=rs_recv.at[o, phase, slot], device_id=moved(axis, shift), device_id_type=MESH,
         )
-
-    def ring_counts(axis):
-        n = size[axis]
-        return n // 2, n - 1 - n // 2
 
     def one_step(step, carry):
         residual = res_ref[...]
@@ -130,59 +141,75 @@
             gathered[o][where_at(())] = block
 
         sends = []
+
+        def begin(copies):
+            for copy in copies.values():
+                copy.start()
+            sends.extend(copies.values())
+            return copies
+
+        waits = {}
         for phase in range(2):
-            flying = []
-            for o in range(3):
-                if phase:
-                    for copy in waits[o]:
-                        copy.wait_recv()
+            for o in SEQUENCE:
+                for copy in waits.get(o, {}).values():
+                    copy.wait_recv()
                 axis, full = ORDERS[o][phase], ORDERS[o][:phase]
-                flying.append([
-                    ag_copy(o, phase, d - 1, axis, full, here[axis], d)
-                    for d in sorted(range(1, size[axis]), key=lambda d: -min(d, size[axis] - d))
-                ])
-                for copy in flying[o]:
-                    copy.start()
-                sends += flying[o]
-            waits = flying
-        rounds = max(size[o[2]] // 2 for o in ORDERS)
-        for t in range(1, rounds + 1):
-            flying = []
-            for o in range(3):
-                for copy in waits[o]:
-                    copy.wait_recv()
-                axis, full = ORDERS[o][2], ORDERS[o][:2]
-                right, left = ring_counts(axis)
-                copies = []
-                if t <= right:
-                    copies.append(ag_copy(o, 2, t - 1, axis, full, away(axis, 1 - t), 1))
-                if t <= left:
-                    copies.append(ag_copy(o, 2, right + t - 1, axis, full, away(axis, t - 1), -1))
-                for copy in copies:
-                    copy.start()
-                sends += copies
-                flying.append(copies)
-            waits = flying
-        for o in range(3):
-            for copy in waits[o]:
+                far = sorted(range(1, size[axis]), key=lambda d: -min(d, size[axis] - d))
+                waits[o] = begin(
+                    {d: ag_copy(o, phase, d - 1, axis, full, here[axis], d) for d in far}
+                )
+        for o in SEQUENCE:
+            for copy in waits[o].values():
                 copy.wait_recv()
+            axis, full = ORDERS[o][2], ORDERS[o][:2]
+            if size[axis] < LONG:
+                waits[o] = begin({
+                    d: ag_copy(o, 2, d - 1, axis, full, here[axis], d)
+                    for d in range(1, size[axis])
+                })
+                continue
+            copies = {}
+            for part in range(2):
+                for base, sign in SIDES:
+                    copies[sign, 2, part] = ag_copy(
+                        o, 2, base + part, axis, full, here[axis], 2 * sign, part
+                    )
+            for base, sign in SIDES:
+                copies[sign, 1] = ag_copy(o, 2, base + 2, axis, full, here[axis], sign)
+            waits[o] = begin(copies)
+        for o in SEQUENCE:
+            axis, full = ORDERS[o][2], ORDERS[o][:2]
+            if size[axis] < LONG:
+                continue
+            for part in range(2):
+                for base, sign in SIDES:
+                    waits[o].pop((sign, 2, part)).wait_recv()
+                    at = away(axis, -2 * sign)
+                    copies = {}
+                    if base == 6 * part:
+                        copies[sign, 4] = ag_copy(o, 2, base + 5, axis, full, at, 2 * sign, part)
+                    copies[sign, 3, part] = ag_copy(o, 2, base + 3 + part, axis, full, at, sign, part)
+                    waits[o].update(begin(copies))
 
         chunk = tokens // size["z"]
         swaps = []
-        for z in range(size["z"]):
-            rows = pl.ds(z * chunk, chunk)
-            total = None
-            for o in range(3):
+        for place, o in enumerate(LANDING):
+            for copy in waits[o].values():
+                copy.wait_recv()
+            for z in range(size["z"]):
+                rows = pl.ds(z * chunk, chunk)
                 x = gathered[o][z].reshape(chunk, gathered[o].shape[-1])[:, : widths[o]]
-                part = jnp.dot(
+                total = jnp.dot(
                     x, wgu_ref[starts[o] : starts[o] + widths[o], :], preferred_element_type=F32
                 )
-                total = part if total is None else total + part
-            gu_ref[rows, :] = total
-            xs_ref[rows, :] = total.astype(BF16)
-            swap = to_mate(xs_ref.at[rows], xr_ref.at[rows], 3 + z)
-            swap.start()
-            swaps.append(swap)
+                if place:
+                    total += gu_ref[rows, :]
+                gu_ref[rows, :] = total
+                if place == 2:
+                    xs_ref[rows, :] = total.astype(BF16)
+                    swap = to_mate(xs_ref.at[rows], xr_ref.at[rows], 3 + z)
+                    swap.start()
+                    swaps.append(swap)
         hidden = wd_ref.shape[0]
         mine = (
             lax.broadcasted_iota(jnp.int32, (tokens, TILE), 1) == rack
@@ -199,93 +226,104 @@
             act_ref[rows, :] = (gate / (1.0 + jnp.exp(-gate)) * up).astype(BF16)
         for copy in sends:
             copy.wait_send()
-        for o in range(3):
+
+        sends = []
+        waits = {}
+        for o in SEQUENCE:
             part = jnp.dot(
                 act_ref[...], wd_ref[:, starts[o] : starts[o] + widths[o]],
                 preferred_element_type=F32,
             )
             partial[o][...] = (part * weight).astype(BF16).reshape(partial[o].shape)
-
-        sends = []
-        waits = [[], [], []]
-        for t in range(1, rounds + 1):
-            flying = []
-            for o in range(3):
-                axis, full = ORDERS[o][2], ORDERS[o][:2]
-                right, left = ring_counts(axis)
-                copies = []
-                for count, base, sign in ((right, 0, 1), (left, right, -1)):
-                    if t > count:
-                        continue
-                    slot = base + t - 1
-                    at = where_at(full, axis, away(axis, sign * (count - t + 1)))
-                    if t == 1:
-                        src = partial[o].at[at]
-                    else:
-                        waits[o][0 if sign > 0 else 1].wait_recv()
-                        ring_out[o][slot] = ring_in[o][slot - 1] + partial[o][at]
-                        src = ring_out[o].at[slot]
-                    copy = rs_copy(o, 0, slot, src, ring_in[o].at[slot], axis, sign)
-                    copy.start()
-                    copies.append(copy)
-                sends += copies
-                if waits[o] and len(copies) < len(waits[o]):
-                    copies = copies + waits[o][len(copies):]
-                flying.append(copies)
-            waits = flying
-        for o in range(3):
             axis, full = ORDERS[o][2], ORDERS[o][:2]
-            right, left = ring_counts(axis)
-            for copy in waits[o]:
+            if size[axis] < LONG:
+                waits[o] = begin({
+                    d: rs_copy(
+                        o, 0, d - 1, partial[o].at[where_at(full, axis, away(axis, d))],
+                        ring_in[o].at[d - 1], axis, d,
+                    )
+                    for d in range(1, size[axis])
+                })
+                continue
+            copies = {}
+            for side, (base, sign) in enumerate(SIDES):
+                copies[sign, 4] = rs_copy(
+                    o, 0, base + 2, partial[o].at[where_at(full, axis, away(axis, 4 * sign), side)],
+                    ring_in[o].at[(side, 1) + inner(full, side)], axis, 2 * sign,
+                )
+            for half_part in range(2):
+                for side, (base, sign) in enumerate(SIDES):
+                    p = half_part if side == 0 else 1 - half_part
+                    copies[sign, 3, p] = rs_copy(
+                        o, 0, base + p,
+                        partial[o].at[where_at(full, axis, away(axis, 3 * sign), p)],
+                        ring_in[o].at[(side, 0) + inner(full, p)], axis, sign,
+                    )
+            for side, (base, sign) in enumerate(SIDES):
+                copies[sign, 1] = rs_copy(
+                    o, 0, base + 3, partial[o].at[where_at(full, axis, away(axis, sign))],
+                    ring_in[o].at[side, 2], axis, sign,
+                )
+            waits[o] = begin(copies)
+        for o in SEQUENCE:
+            axis, full = ORDERS[o][2], ORDERS[o][:2]
+            if size[axis] < LONG:
+                continue
+            for half_part in range(2):
+                for side, (base, sign) in enumerate(SIDES):
+                    p = half_part if side == 0 else 1 - half_part
+                    block = inner(full, p)
+                    waits[o].pop((sign, 3, p)).wait_recv()
+                    total = partial[o][where_at(full, axis, away(axis, 2 * sign), p)].astype(F32)
+                    total += ring_in[o][(side, 0) + block].astype(F32)
+                    if p == side:
+                        waits[o].pop((sign, 4)).wait_recv()
+                        total += ring_in[o][(side, 1) + block].astype(F32)
+                    ring_out[o][(side,) + block] = total.astype(BF16)
+                    waits[o].update(begin({(sign, 2, p): rs_copy(
+                        o, 0, base + 4 + p, ring_out[o].at[(side,) + block],
+                        ring_in[o].at[(side, 3) + block], axis, 2 * sign,
+                    )}))
+        flying = {}
+        for o in LANDING:
+            axis, full = ORDERS[o][2], ORDERS[o][:2]
+            for copy in waits[o].values():
                 copy.wait_recv()
             total = partial[o][where_at(full, axis, here[axis])].astype(F32)
-            total += ring_in[o][right - 1].astype(F32)
-            if left:
-                total += ring_in[o][right + left - 1].astype(F32)
+            if size[axis] < LONG:
+                for d in range(1, size[axis]):
+                    total += ring_in[o][d - 1].astype(F32)
+            else:
+                for side in range(2):
+                    total += ring_in[o][side, 2].astype(F32) + ring_in[o][side, 3].astype(F32)
             mid_out[o][...] = total.astype(BF16)
-
-        flying = []
-        for o in range(3):
             axis = ORDERS[o][1]
-            other = [a for a in STORED if a in ORDERS[o][:2]]
-            copies = []
+            copies = {}
             for d in range(1, size[axis]):
-                at = tuple(
-                    away(axis, d) if a == axis else pl.ds(0, size[a]) for a in other
-                )
-                copies.append(
-                    rs_copy(o, 1, d - 1, mid_out[o].at[at], mid_in[o].at[d - 1], axis, d)
-                )
-            for copy in copies:
-                copy.start()
-            sends += copies
-            flying.append(copies)
+                at = tuple(away(axis, d) if a == axis else pl.ds(0, size[a]) for a in STORED if a in full)
+                copies[d] = rs_copy(o, 1, d - 1, mid_out[o].at[at], mid_in[o].at[d - 1], axis, d)
+            flying[o] = begin(copies)
         waits = flying
-        flying = []
-        for o in range(3):
-            axis = ORDERS[o][1]
-            other = [a for a in STORED if a in ORDERS[o][:2]]
-            at = tuple(here[axis] if a == axis else pl.ds(0, size[a]) for a in other)
+        flying = {}
+        for o in LANDING:
+            axis, full = ORDERS[o][1], ORDERS[o][:2]
+            at = tuple(here[axis] if a == axis else pl.ds(0, size[a]) for a in STORED if a in full)
             total = mid_out[o][at].astype(F32)
             for d in range(1, size[axis]):
-                waits[o][d - 1].wait_recv()
+                waits[o][d].wait_recv()
                 total += mid_in[o][d - 1].astype(F32)
             last_out[o][...] = total.astype(BF16)
             axis = ORDERS[o][0]
-            copies = [
-                rs_copy(o, 2, d - 1, last_out[o].at[away(axis, d)], last_in[o].at[d - 1], axis, d)
+            flying[o] = begin({
+                d: rs_copy(o, 2, d - 1, last_out[o].at[away(axis, d)], last_in[o].at[d - 1], axis, d)
                 for d in range(1, size[axis])
-            ]
-            for copy in copies:
-                copy.start()
-            sends += copies
-            flying.append(copies)
+            })
         waits = flying
-        for o in range(3):
+        for o in LANDING:
             axis = ORDERS[o][0]
             total = last_out[o][here[axis]].astype(F32)
             for d in range(1, size[axis]):
-                waits[o][d - 1].wait_recv()
+                waits[o][d].wait_recv()
                 total += last_in[o][d - 1].astype(F32)
             res_ref[:, starts[o] : starts[o] + widths[o]] += total
         for copy in sends:
@@ -335,17 +373,18 @@
         pltpu.VMEM((2, TILE), F32),
         pltpu.VMEM((2, TILE), F32),
     ]
-    for _ in range(2):
-        scratch += [
-            pltpu.VMEM((size[o[2]] - 1,) + dims(o[:2]) + (2, w), BF16) for o, w in zip(ORDERS, widths)
-        ]
+    lines = [(2, 4) if size[o[2]] >= LONG else (size[o[2]] - 1,) for o in ORDERS]
+    scratch += [
+        pltpu.VMEM(n + dims(o[:2]) + (2, w), BF16) for n, o, w in zip(lines, ORDERS, widths)
+    ]
+    scratch += [pltpu.VMEM((2,) + dims(o[:2]) + (2, w), BF16) for o, w in zip(ORDERS, widths)]
     scratch += [pltpu.VMEM(dims(o[:2]) + (2, w), BF16) for o, w in zip(ORDERS, widths)]
     scratch += [
         pltpu.VMEM((size[o[1]] - 1, size[o[0]], 2, w), BF16) for o, w in zip(ORDERS, widths)
     ]
     scratch += [pltpu.VMEM((size[o[0]], 2, w), BF16) for o, w in zip(ORDERS, widths)]
     scratch += [pltpu.VMEM((size[o[0]] - 1, 2, w), BF16) for o, w in zip(ORDERS, widths)]
-    most = max(grid) - 1
+    most = 12
     scratch += [pltpu.SemaphoreType.DMA((3, 3, most))] * 4
     scratch += [pltpu.SemaphoreType.DMA((3 + size["z"],))] * 2
     return pl.pallas_call(

time: 278 us -> 218 us (0.78)
  Pallas kernels: 274 us -> 214 us
    pallas_call x1, Pallas kernels: 274 us -> 214 us  [per_device(): pl.pallas_call(functools.partial(kernel, grid, steps, top, 0, widths), ou...]
where the time goes in v2:
time: 218 us
  Pallas kernels  214 us (98%)
  local copies, waits for them, and re-layouts  3.31 us (2%)
    pallas_call x1, Pallas kernels, per_device(): pl.pallas_call(functools.partial(kernel, grid, steps, top, 0, widths), ou...  214 us

profile of v2, /device:TPU:1, one launch (start us, length us, event | category | flops | bytes accessed | tf_op | source)
XLA Modules:
  0.0 217.7 jit_solution(12146211443535913)
XLA Ops:
  0.0 0.7 reshape.3.gain_ref
  0.7 0.0 copy-start
  0.7 0.0 copy-start.1
  0.8 0.0 copy-start.2
  0.8 0.0 copy-start.3
  0.8 2.0 copy.7
  2.7 0.0 copy-done
  2.8 0.0 copy-done.1
  2.8 0.0 copy-done.2
  2.8 0.0 copy-done.3
  2.8 214.3 %shard_map.64 = f32[1,3584]{1,0:T(1,128)S(1)} custom-call(bf16[1,3584]{1,0:T(2,128)(2,1)S(1)} %copy-done.1, f32[1,3584]{1,0:T(1,128)S(1)} %reshape.3.gain_ref, s32[4,8]{1,0:T(4,128)S(1)} %bitcast.8, s32[4,8]{1,0:T(4,128)S(1)} %bitcast.9, bf16[1792,512]{1,0:T(8,128)(2,1)S(1)} %bitcast.6, bf16[256,1792]{1,0:T(8,128)(2,1)S(1)} %bitcast.7), custom_call_target="tpu_custom_call" | custom-call | tf_op jit(solution)/shard_map/pallas_call | solution.py:390
  217.1 0.6 copy.9
Async XLA Ops:
  0.7 2.0 copy-start
  0.7 2.0 copy-start.1
  0.8 2.0 copy-start.2
  0.8 2.0 copy-start.3

commit v3 on v2

--- a/solution.py
+++ b/solution.py
@@ -18,19 +18,20 @@
 SIDES = ((0, 1), (6, -1))
 SEQUENCE = (0, 2, 1)
 LANDING = (1, 0, 2)
+TAGGED = LANDING[-1]
 
 
 def shares_of(tiles):
     first = (tiles + 1) // 3
     second = (tiles + 1 - first) // 2
-    return (first - 1, second, tiles + 1 - first - second)
+    return (first, second, tiles - first - second)
 
 
 def kernel(
-    grid, steps, top, experts, widths,
+    grid, steps, top, widths,
     hid_ref, gain_ref, ids_ref, lev_ref, wgu_ref, wd_ref, out_ref,
     ga, gb, gc, pa, pb, pc, gu_ref, act_ref, xs_ref, xr_ref,
-    res_ref, mix_ref, mixs_ref, mixr_ref, hs_ref, hr_ref, fs_ref, fr_ref, sss_ref, ssr_ref,
+    res_ref, mix_ref, mixs_ref, mixr_ref, hs_ref, hr_ref, fs_ref, fr_ref, tag_ref,
     rr_a, rr_b, rr_c, st_a, st_b, st_c, u_a, u_b, u_c, v_a, v_b, v_c, w_a, w_b, w_c, t_a, t_b, t_c,
     ag_send, ag_recv, rs_send, rs_recv, pair_send, pair_recv,
 ):
@@ -39,6 +40,7 @@
     here = {"x": rack // size["y"], "y": rack % size["y"], "z": col // 2}
     core = col % 2
     half = sum(widths)
+    experts = grid[0] * grid[1]
     tokens = 2 * grid[0] * grid[1] * grid[2]
     starts = (0, widths[0], widths[0] + widths[1])
     gathered, partial = (ga, gb, gc), (pa, pb, pc)
@@ -74,9 +76,10 @@
         spans = span(full, part)
         return tuple(spans[a] for a in STORED if a in full)
 
-    def to_mate(src, dst, slot):
+    def to_mate(src, dst, slot, turn=0):
         return pltpu.make_async_remote_copy(
-            src_ref=src, dst_ref=dst, send_sem=pair_send.at[slot], recv_sem=pair_recv.at[slot],
+            src_ref=src, dst_ref=dst, send_sem=pair_send.at[turn, slot],
+            recv_sem=pair_recv.at[turn, slot],
             device_id=mate, device_id_type=MESH,
         )
 
@@ -124,22 +127,33 @@
             recv_sem=rs_recv.at[o, phase, slot], device_id=moved(axis, shift), device_id_type=MESH,
         )
 
+    def first_copies(o):
+        axis = ORDERS[o][0]
+        far = sorted(range(1, size[axis]), key=lambda d: -min(d, size[axis] - d))
+        return {d: ag_copy(o, 0, d - 1, axis, (), here[axis], d) for d in far}
+
+    def send_share(o, step):
+        cols = slice(starts[o], starts[o] + widths[o])
+        block = (res_ref[:, cols] * gain[:, cols]).astype(BF16)
+        if o == TAGGED:
+            residual = res_ref[...]
+            square = jnp.sum(residual * residual, axis=-1, keepdims=True)
+            tag = mix_ref[step]
+            lane = lax.broadcasted_iota(jnp.int32, (2, TILE), 1)
+            for n in range(3):
+                piece = square.astype(BF16).astype(F32)
+                tag = jnp.where(lane == experts + n, piece, tag)
+                square = square - piece
+            block = jnp.concatenate([block, tag.astype(BF16)], axis=1)
+        gathered[o][where_at(())] = block
+        for copy in first_copies(o).values():
+            copy.start()
+
+    for o in LANDING:
+        send_share(o, 0)
+
     def one_step(step, carry):
-        residual = res_ref[...]
-        sss_ref[...] = jnp.broadcast_to(
-            jnp.sum(residual * residual, axis=-1, keepdims=True), sss_ref.shape
-        )
-        copy = to_mate(sss_ref, ssr_ref, 2)
-        copy.start()
-        copy.wait()
-        total = (sss_ref[...] + ssr_ref[...])[:, :1]
-        normed = (residual * lax.rsqrt(total / (2 * half) + 1e-6) * gain).astype(BF16)
-        for o in range(3):
-            block = normed[:, starts[o] : starts[o] + widths[o]]
-            if o == 0:
-                block = jnp.concatenate([block, mix_ref[step].astype(BF16)], axis=1)
-            gathered[o][where_at(())] = block
-
+        turn = lax.rem(step, 2)
         sends = []
 
         def begin(copies):
@@ -148,16 +162,15 @@
             sends.extend(copies.values())
             return copies
 
-        waits = {}
-        for phase in range(2):
-            for o in SEQUENCE:
-                for copy in waits.get(o, {}).values():
-                    copy.wait_recv()
-                axis, full = ORDERS[o][phase], ORDERS[o][:phase]
-                far = sorted(range(1, size[axis]), key=lambda d: -min(d, size[axis] - d))
-                waits[o] = begin(
-                    {d: ag_copy(o, phase, d - 1, axis, full, here[axis], d) for d in far}
-                )
+        waits = {o: first_copies(o) for o in range(3)}
+        for o in LANDING:
+            sends.extend(waits[o].values())
+        for o in LANDING:
+            for copy in waits[o].values():
+                copy.wait_recv()
+            axis, full = ORDERS[o][1], ORDERS[o][:1]
+            far = sorted(range(1, size[axis]), key=lambda d: -min(d, size[axis] - d))
+            waits[o] = begin({d: ag_copy(o, 1, d - 1, axis, full, here[axis], d) for d in far})
         for o in SEQUENCE:
             for copy in waits[o].values():
                 copy.wait_recv()
@@ -196,6 +209,10 @@
         for place, o in enumerate(LANDING):
             for copy in waits[o].values():
                 copy.wait_recv()
+            if o == TAGGED:
+                spot = (slice(None),) * 4 + (pl.ds(widths[o], TILE),)
+                told = to_mate(gathered[o].at[spot], tag_ref.at[turn], 3 + size["z"], turn)
+                told.start()
             for z in range(size["z"]):
                 rows = pl.ds(z * chunk, chunk)
                 x = gathered[o][z].reshape(chunk, gathered[o].shape[-1])[:, : widths[o]]
@@ -207,21 +224,26 @@
                 gu_ref[rows, :] = total
                 if place == 2:
                     xs_ref[rows, :] = total.astype(BF16)
-                    swap = to_mate(xs_ref.at[rows], xr_ref.at[rows], 3 + z)
+                    swap = to_mate(xs_ref.at[rows], xr_ref.at[turn, rows], 3 + z, turn)
                     swap.start()
                     swaps.append(swap)
         hidden = wd_ref.shape[0]
-        mine = (
-            lax.broadcasted_iota(jnp.int32, (tokens, TILE), 1) == rack
-        )
-        weight = jnp.sum(
-            jnp.where(mine, ga[..., widths[0] :].reshape(tokens, TILE).astype(F32), 0.0),
-            axis=-1, keepdims=True,
-        )
+        lane = lax.broadcasted_iota(jnp.int32, (tokens, TILE), 1)
+        square = (lane >= experts) & (lane < experts + 3)
+
+        def picked(tag, mask):
+            return jnp.sum(jnp.where(mask, tag, 0.0), axis=-1, keepdims=True)
+
+        tag = gathered[TAGGED][..., widths[TAGGED] :].reshape(tokens, TILE).astype(F32)
+        weight = picked(tag, lane == rack)
+        told.wait()
+        total = picked(tag, square) + picked(tag_ref[turn].reshape(tokens, TILE).astype(F32), square)
+        scale = lax.rsqrt(total / (2 * half) + 1e-6)
         for z in range(size["z"]):
             rows = pl.ds(z * chunk, chunk)
             swaps[z].wait()
-            both = gu_ref[rows, :] + xr_ref[rows, :].astype(F32)
+            both = gu_ref[rows, :] + xr_ref[turn, rows, :].astype(F32)
+            both = both * scale[z * chunk : (z + 1) * chunk]
             gate, up = both[:, :hidden], both[:, hidden:]
             act_ref[rows, :] = (gate / (1.0 + jnp.exp(-gate)) * up).astype(BF16)
         for copy in sends:
@@ -326,6 +348,11 @@
                 waits[o][d].wait_recv()
                 total += last_in[o][d - 1].astype(F32)
             res_ref[:, starts[o] : starts[o] + widths[o]] += total
+
+            @pl.when(step < steps - 1)
+            def _(o=o):
+                send_share(o, step + 1)
+
         for copy in sends:
             copy.wait_send()
         return carry
@@ -355,13 +382,13 @@
     def dims(names):
         return tuple(size[a] for a in STORED if a in names)
 
-    scratch = [pltpu.VMEM(stored + (2, w + (TILE if o == 0 else 0)), BF16) for o, w in enumerate(widths)]
+    scratch = [pltpu.VMEM(stored + (2, w + (TILE if o == TAGGED else 0)), BF16) for o, w in enumerate(widths)]
     scratch += [pltpu.VMEM(stored + (2, w), BF16) for w in widths]
     scratch += [
         pltpu.VMEM((tokens, 2 * hidden), F32),
         pltpu.VMEM((tokens, hidden), BF16),
         pltpu.VMEM((tokens, 2 * hidden), BF16),
-        pltpu.VMEM((tokens, 2 * hidden), BF16),
+        pltpu.VMEM((2, tokens, 2 * hidden), BF16),
         pltpu.VMEM((2, half), F32),
         pltpu.VMEM((steps, 2, TILE), F32),
         pltpu.VMEM((steps, TILE), F32),
@@ -370,8 +397,7 @@
         pltpu.VMEM((1, half), F32),
         pltpu.VMEM((1, half), F32),
         pltpu.VMEM((1, half), F32),
-        pltpu.VMEM((2, TILE), F32),
-        pltpu.VMEM((2, TILE), F32),
+        pltpu.VMEM((2,) + stored + (2, TILE), BF16),
     ]
     lines = [(2, 4) if size[o[2]] >= LONG else (size[o[2]] - 1,) for o in ORDERS]
     scratch += [
@@ -386,9 +412,9 @@
     scratch += [pltpu.VMEM((size[o[0]] - 1, 2, w), BF16) for o, w in zip(ORDERS, widths)]
     most = 12
     scratch += [pltpu.SemaphoreType.DMA((3, 3, most))] * 4
-    scratch += [pltpu.SemaphoreType.DMA((3 + size["z"],))] * 2
+    scratch += [pltpu.SemaphoreType.DMA((2, 4 + size["z"]))] * 2
     return pl.pallas_call(
-        functools.partial(kernel, grid, steps, top, 0, widths),
+        functools.partial(kernel, grid, steps, top, widths),
         out_shape=jax.ShapeDtypeStruct((1, width), F32),
         in_specs=[pl.BlockSpec(memory_space=pltpu.VMEM)] * 6,
         out_specs=pl.BlockSpec(memory_space=pltpu.VMEM),

time: 218 us -> 210 us (0.963)
  Pallas kernels: 214 us -> 207 us
    pallas_call x1, Pallas kernels: 214 us -> 207 us  [per_device(): pl.pallas_call(functools.partial(kernel, grid, steps, top, widths), out_s...]
where the time goes in v3:
time: 210 us
  Pallas kernels  207 us (99%)
  local copies, waits for them, and re-layouts  3.31 us (2%)
    pallas_call x1, Pallas kernels, per_device(): pl.pallas_call(functools.partial(kernel, grid, steps, top, widths), out_s...  207 us

profile of v3, /device:TPU:1, one launch (start us, length us, event | category | flops | bytes accessed | tf_op | source)
XLA Modules:
  0.0 209.9 jit_solution(4044728165170092884)
XLA Ops:
  0.0 0.7 reshape.3.gain_ref
  0.7 0.0 copy-start
  0.7 0.0 copy-start.1
  0.8 0.0 copy-start.2
  0.8 0.0 copy-start.3
  0.8 2.0 copy.7
  2.7 0.0 copy-done
  2.8 0.0 copy-done.1
  2.8 0.0 copy-done.2
  2.8 0.0 copy-done.3
  2.8 206.6 %shard_map.64 = f32[1,3584]{1,0:T(1,128)S(1)} custom-call(bf16[1,3584]{1,0:T(2,128)(2,1)S(1)} %copy-done.1, f32[1,3584]{1,0:T(1,128)S(1)} %reshape.3.gain_ref, s32[4,8]{1,0:T(4,128)S(1)} %bitcast.8, s32[4,8]{1,0:T(4,128)S(1)} %bitcast.9, bf16[1792,512]{1,0:T(8,128)(2,1)S(1)} %bitcast.6, bf16[256,1792]{1,0:T(8,128)(2,1)S(1)} %bitcast.7), custom_call_target="tpu_custom_call" | custom-call | tf_op jit(solution)/shard_map/pallas_call | solution.py:416
  209.3 0.6 copy.9
Async XLA Ops:
  0.7 2.0 copy-start
  0.7 2.0 copy-start.1
  0.8 2.0 copy-start.2
  0.8 2.0 copy-start.3

commit v4 on v3

--- a/solution.py
+++ b/solution.py
@@ -190,11 +190,11 @@
             for base, sign in SIDES:
                 copies[sign, 1] = ag_copy(o, 2, base + 2, axis, full, here[axis], sign)
             waits[o] = begin(copies)
-        for o in SEQUENCE:
-            axis, full = ORDERS[o][2], ORDERS[o][:2]
-            if size[axis] < LONG:
-                continue
-            for part in range(2):
+        for part in range(2):
+            for o in SEQUENCE:
+                axis, full = ORDERS[o][2], ORDERS[o][:2]
+                if size[axis] < LONG:
+                    continue
                 for base, sign in SIDES:
                     waits[o].pop((sign, 2, part)).wait_recv()
                     at = away(axis, -2 * sign)
@@ -287,11 +287,11 @@
                     ring_in[o].at[side, 2], axis, sign,
                 )
             waits[o] = begin(copies)
-        for o in SEQUENCE:
-            axis, full = ORDERS[o][2], ORDERS[o][:2]
-            if size[axis] < LONG:
-                continue
-            for half_part in range(2):
+        for half_part in range(2):
+            for o in SEQUENCE:
+                axis, full = ORDERS[o][2], ORDERS[o][:2]
+                if size[axis] < LONG:
+                    continue
                 for side, (base, sign) in enumerate(SIDES):
                     p = half_part if side == 0 else 1 - half_part
                     block = inner(full, p)

time: 210 us -> 210 us (level)
  no operation moved by 1% of the time
where the time goes in v4:
time: 210 us; the launch traced here: 209 us
  Pallas kernels  206 us (98%)
  local copies, waits for them, and re-layouts  3.31 us (2%)
    pallas_call x1, Pallas kernels, per_device(): pl.pallas_call(functools.partial(kernel, grid, steps, top, widths), out_s...  206 us

profile of v4, /device:TPU:1, one launch (start us, length us, event | category | flops | bytes accessed | tf_op | source)
XLA Modules:
  0.0 209.4 jit_solution(4322108242785417059)
XLA Ops:
  0.0 0.7 reshape.3.gain_ref
  0.7 0.0 copy-start
  0.7 0.0 copy-start.1
  0.8 0.0 copy-start.2
  0.8 0.0 copy-start.3
  0.8 2.0 copy.7
  2.7 0.0 copy-done
  2.8 0.0 copy-done.1
  2.8 0.0 copy-done.2
  2.8 0.0 copy-done.3
  2.8 206.0 %shard_map.64 = f32[1,3584]{1,0:T(1,128)S(1)} custom-call(bf16[1,3584]{1,0:T(2,128)(2,1)S(1)} %copy-done.1, f32[1,3584]{1,0:T(1,128)S(1)} %reshape.3.gain_ref, s32[4,8]{1,0:T(4,128)S(1)} %bitcast.8, s32[4,8]{1,0:T(4,128)S(1)} %bitcast.9, bf16[1792,512]{1,0:T(8,128)(2,1)S(1)} %bitcast.6, bf16[256,1792]{1,0:T(8,128)(2,1)S(1)} %bitcast.7), custom_call_target="tpu_custom_call" | custom-call | tf_op jit(solution)/shard_map/pallas_call | solution.py:416
  208.8 0.6 copy.9
Async XLA Ops:
  0.7 2.0 copy-start
  0.7 2.0 copy-start.1
  0.8 2.0 copy-start.2
  0.8 2.0 copy-start.3
